TPU v7x, 32 devices: a whole 2x2x4 slice. The times are simulated.
32 devices in a mesh: dp: 8 (over z, y), group: 4 (over x, core).
Axes of the slice: x: 2, y: 2, z: 4, core: 2. Of those that a mesh axis runs over, the one named last changes fastest.
Arguments:
- waveform: bfloat16 [128, 2560], P(('dp', 'group')), may hold values from -6 to 6
- lengths: int32 [128], P(('dp', 'group')), may hold values from 1280 to 2560
- packing: int32 [128], P(('dp', 'group')), may hold values from 0 to 15, as said below
- first_weight: bfloat16 [512, 10], P('dp'), may hold values from -2 to 2
- norm_gain: float32 [512], replicated, may hold values from 0.25 to 1.75
- norm_bias: float32 [512], replicated, may hold values from -3 to 3
- conv_weight: bfloat16 [512, 1536], P('dp'), may hold values from -0.15625 to 0.15625
- grad_features: bfloat16 [128, 255, 512], P(('dp', 'group')), may hold values from -0.25 to 0.25
Outputs:
- features: bfloat16 [128, 255, 512], P(('dp', 'group'))
- grad_conv: float32 [512, 1536], P('dp')
- grad_first: float32 [512, 10], P('dp')
- grad_gain: float32 [512], replicated
- grad_bias: float32 [512], replicated
Inputs may be any that keep to these rules, and one draw needn't show every extreme that they name: `packing`: within each index of dp the 16 rows form a permutation of the positions of that index's block; position p lies on the device of group index p // 4 of the same dp index. Each device sends an even number of its rows to each device of its group, at most 2 to one device, and exactly 2 to some.
All inputs are finite; a program needn't handle non-finite values.
Results may differ from a plain program's by a relative error of at most 0.0057.
Values may be sent and summed in bfloat16 or wider, within the bound.
A program may use at most 64 MiB of HBM per device.

v0:
```python
import jax
import jax.numpy as jnp
from jax import lax
from jax.sharding import PartitionSpec as P


def gelu_slope(values):
    return (
        0.5 * (1.0 + lax.erf(values * 0.7071067811865476))
        + values * jnp.exp(-0.5 * values * values) * 0.3989422804014327
    )


def tap_matrix(hidden, frames_second):
    row_count, frames_first, channels = hidden.shape
    zero_frame = jnp.zeros((row_count, 1, channels), hidden.dtype)
    paired = jnp.concatenate([hidden, zero_frame], axis=1).reshape(
        row_count, frames_second + 1, 2, channels
    )
    even_half = paired[:, :, 0]
    odd_half = paired[:, :, 1]
    stacked = jnp.concatenate(
        [even_half[:, :frames_second], odd_half[:, :frames_second], even_half[:, 1:]], axis=2
    )
    return stacked.reshape(row_count * frames_second, 3 * channels)


def spread_back(back_taps, row_count, frames_second, frames_first):
    first_tap = back_taps[0].reshape(row_count, frames_second, -1)
    middle_tap = back_taps[1].reshape(row_count, frames_second, -1)
    last_tap = back_taps[2].reshape(row_count, frames_second, -1)
    channels = first_tap.shape[2]
    zero_frame = jnp.zeros((row_count, 1, channels), jnp.float32)
    even_half = jnp.concatenate([first_tap, zero_frame], axis=1) + jnp.concatenate(
        [zero_frame, last_tap], axis=1
    )
    odd_half = jnp.concatenate([middle_tap, zero_frame], axis=1)
    joined = jnp.stack([even_half, odd_half], axis=2).reshape(
        row_count, 2 * frames_second + 2, channels
    )
    return joined[:, :frames_first]


def local(
    waveform, lengths, packing, first_weight, norm_gain, norm_bias, conv_weight, grad_features
):
    row_count, capacity = waveform.shape
    channels = norm_gain.shape[0]
    frames_first = capacity // 5 - 1
    frames_second = (capacity // 5 - 2) // 2
    groups = lax.axis_size("group")
    own_group = lax.axis_index("group")
    group_rows = groups * row_count
    all_pack, all_lengths = (
        lax.all_gather(packing, "group", axis=0, tiled=True),
        lax.all_gather(lengths, "group", axis=0, tiled=True),
    )
    target = all_pack // row_count
    slot_index = all_pack % row_count
    positions = jnp.arange(group_rows)
    source = positions // row_count
    same_source = source[:, None] == source[None, :]
    same_target = target[:, None] == target[None, :]
    before = positions[:, None] > positions[None, :]
    rank_among = jnp.sum((same_source & same_target & before).astype(jnp.int32), axis=1)
    arriving = target == own_group
    slot_ids = jnp.arange(row_count)
    choose_slot = (slot_index[None, :] == slot_ids[:, None]) & arriving[None, :]
    local_lengths = jnp.sum(jnp.where(choose_slot, all_lengths[None, :], 0), axis=1)
    per_peer = 2 * ((row_count + 2 * groups - 1) // (2 * groups))
    lane_ids = jnp.arange(per_peer)
    own_target = lax.dynamic_slice_in_dim(target, own_group * row_count, row_count)
    own_rank = lax.dynamic_slice_in_dim(rank_among, own_group * row_count, row_count)
    outgoing = (
        (own_target[None, None, :] == jnp.arange(groups)[:, None, None])
        & (own_rank[None, None, :] == lane_ids[None, :, None])
    ).astype(jnp.bfloat16)
    send_rows = jnp.einsum(
        "gkr,rs->gks", outgoing, waveform, preferred_element_type=jnp.float32
    ).astype(jnp.bfloat16)
    received = lax.all_to_all(send_rows, "group", split_axis=0, concat_axis=0, tiled=True)
    pick_slots = (
        choose_slot[:, :, None] & (rank_among[None, :, None] == lane_ids[None, None, :])
    ).astype(jnp.float32)
    pick_slots = jnp.sum(pick_slots.reshape(row_count, groups, row_count, per_peer), axis=2).astype(
        jnp.bfloat16
    )
    wave_rows = jnp.einsum(
        "lsk,skn->ln", pick_slots, received, preferred_element_type=jnp.float32
    ).astype(jnp.bfloat16)
    first_whole = lax.all_gather(first_weight, "dp", axis=0, tiled=True)
    in_length = jnp.arange(capacity)[None, :] < local_lengths[:, None]
    masked = jnp.where(in_length, wave_rows, jnp.zeros_like(wave_rows))
    blocks = masked.reshape(row_count, capacity // 5, 5)
    taps_first = jnp.concatenate([blocks[:, :-1], blocks[:, 1:]], axis=2).reshape(
        row_count * frames_first, 10
    )
    conv_first = lax.dot_general(
        taps_first, first_whole, (((1,), (1,)), ((), ())), preferred_element_type=jnp.float32
    )
    conv_first = conv_first.reshape(row_count, frames_first, channels)
    count_first = (local_lengths - 10) // 5 + 1
    count_second = (count_first - 3) // 2 + 1
    valid_first = (jnp.arange(frames_first)[None, :] < count_first[:, None]).astype(jnp.float32)[
        :, :, None
    ]
    valid_second = (jnp.arange(frames_second)[None, :] < count_second[:, None]).astype(jnp.float32)[
        :, :, None
    ]
    count_float = count_first.astype(jnp.float32)[:, None, None]
    row_mean = jnp.sum(conv_first * valid_first, axis=1, keepdims=True) / count_float
    centred = (conv_first - row_mean) * valid_first
    row_var = jnp.sum(centred * centred, axis=1, keepdims=True) / count_float
    inv_scale = lax.rsqrt(row_var + 1e-05)
    normed = (conv_first - row_mean) * inv_scale
    shifted = normed * norm_gain + norm_bias
    hidden = (jax.nn.gelu(shifted, approximate=False) * valid_first).astype(jnp.bfloat16)
    taps_second = tap_matrix(hidden, frames_second)
    conv_whole = lax.all_gather(conv_weight, "dp", axis=0, tiled=True)
    conv_second = lax.dot_general(
        taps_second, conv_whole, (((1,), (1,)), ((), ())), preferred_element_type=jnp.float32
    )
    conv_second = conv_second.reshape(row_count, frames_second, channels)
    features = (jax.nn.gelu(conv_second, approximate=False) * valid_second).astype(jnp.bfloat16)
    delta_second = (
        grad_features.astype(jnp.float32) * valid_second * gelu_slope(conv_second)
    ).astype(jnp.bfloat16)
    delta_flat = delta_second.reshape(row_count * frames_second, channels)
    back_taps = tuple(
        (
            jnp.dot(
                delta_flat,
                conv_whole[:, tap_index * channels : (tap_index + 1) * channels],
                preferred_element_type=jnp.float32,
            )
            for tap_index in range(3)
        )
    )
    share = lax.psum_scatter(
        lax.dot_general(
            delta_flat, taps_second, (((0,), (0,)), ((), ())), preferred_element_type=jnp.float32
        ),
        "dp",
        scatter_dimension=0,
        tiled=True,
    )
    grad_conv = lax.psum(share, "group")
    delta_hidden = spread_back(back_taps, row_count, frames_second, frames_first)
    delta_norm = delta_hidden * valid_first * gelu_slope(shifted)
    gain_term = jnp.sum(delta_norm * normed, axis=(0, 1))
    bias_term = jnp.sum(delta_norm, axis=(0, 1))
    scaled = delta_norm * norm_gain
    mean_grad = jnp.sum(scaled, axis=1, keepdims=True) / count_float
    mean_cross = jnp.sum(scaled * normed, axis=1, keepdims=True) / count_float
    delta_first = ((scaled - mean_grad - normed * mean_cross) * inv_scale * valid_first).astype(
        jnp.bfloat16
    )
    first_term = lax.dot_general(
        delta_first.reshape(row_count * frames_first, channels),
        taps_first,
        (((0,), (0,)), ((), ())),
        preferred_element_type=jnp.float32,
    )
    stacked = jnp.concatenate([first_term, gain_term[:, None], bias_term[:, None]], axis=1)
    summed = lax.psum(stacked, ("dp", "group"))
    shard_rows = channels // lax.axis_size("dp")
    grad_first = lax.dynamic_slice_in_dim(
        summed[:, :10], lax.axis_index("dp") * shard_rows, shard_rows, 0
    )
    return (features, grad_conv, grad_first, summed[:, 10], summed[:, 11])


def solution(mesh):
    return jax.shard_map(
        local,
        mesh=mesh,
        in_specs=(
            P(("dp", "group"), None),
            P(("dp", "group")),
            P(("dp", "group")),
            P("dp", None),
            P(),
            P(),
            P("dp", None),
            P(("dp", "group"), None, None),
        ),
        out_specs=(P(("dp", "group"), None, None), P("dp", None), P("dp", None), P(), P()),
        check_vma=False,
    )
```

profile of v0, /device:TPU:0, one launch (start us, length us, event | category | flops | bytes accessed | tf_op | source)
XLA Modules:
  0.0 210.4 jit_solution(2185405149943320980)
XLA Ops:
  7.9 1.2 dynamic-slice
  9.8 0.9 dynamic-update-slice
  11.5 6.4 %all-reduce.6 = (s32[16]{0:T(128)S(1)}, s32[16]{0:T(128)S(1)}) all-reduce(s32[16]{0:T(128)S(1)} %dynamic-update-slice, s32[16]{0:T(128)S(1)} %dynamic-update-slice.1), channel_id=1, replica_groups=mesh['dp'=8,'group'=4] {'group'}, use_global_device_ids=true, to_apply=%add.4 | all-reduce | flops 32 | bytes 256
  19.1 3.3 %all-to-all-start = ((bf16[4,2,2560]{2,1,0:T(2,128)(2,1)}), bf16[4,2,2560]{2,1,0:T(2,128)(2,1)S(1)}, u32[]{:S(2)}, u32[]{:S(2)}) async-start(bf16[4,2,2560]{2,1,0:T(2,128)(2,1)} %copy.42), calls=%async_computation | async-start | bytes 81920 | tf_op jit(solution)/shard_map/all_to_all | solution.py:81
  23.2 31.5 %all-gather = bf16[8,64,10]{1,2,0:T(8,128)(2,1)S(1)} all-gather(bf16[1,64,10]{1,2,0:T(8,128)(2,1)} %bitcast.60), channel_id=1, replica_groups=mesh['dp'=8,'group'=4] {'dp'}, dimensions={0}, use_global_device_ids=true | all-gather | bytes 11520 | tf_op jit(solution)/shard_map/all_gather | solution.py:91
  55.1 1.0 reshape.327
  56.8 1.0 multiply_reduce_fusion.3
  58.7 10.2 %fusion.3 = bf16[4,511,512]{2,1,0:T(8,128)(2,1)S(1)} fusion(f32[4,511,512]{2,1,0:T(8,128)S(1)} %get-tuple-element.51, f32[512]{0:T(512)S(1)} %copy-done.5, f32[512]{0:T(512)S(1)} %copy-done.6, f32[4,512]{1,0:T(4,128)S(1)} %add_rsqrt_fusion, f32[4,512]{1,0:T(4,128)S(1)} %broadcast_divide_fusion.2, f32[4,511]{1,0:T(4,128)S(1)} %fusion.46), kind=kLoop, calls=%fused_computation.5 | loop fusion | flops 73256960 | bytes 6307824 | tf_op jit(solution)/shard_map/convert_element_type | solution.py:117
  68.9 1.5 concatenate.22
  70.4 2.7 %reshape.328 = bf16[4,256,2,512]{3,2,1,0:T(2,128)(2,1)S(1)} reshape(bf16[4,512,512]{2,1,0:T(8,128)(2,1)} %concatenate.22) | data formatting | bytes 4194304 | tf_op jit(solution)/shard_map/reshape | solution.py:17
  73.2 3.0 %fusion.59 = (bf16[4,256,1,512]{3,2,1,0:T(2,128)(2,1)S(1)}, bf16[4,256,1,512]{3,2,1,0:T(2,128)(2,1)S(1)}) fusion(bf16[4,256,2,512]{3,2,1,0:T(2,128)(2,1)S(1)} %reshape.328), kind=kLoop, calls=%fused_computation.134 | loop fusion | bytes 4194304 | tf_op jit(solution)/shard_map/slice | solution.py:21
  76.7 1.3 fusion.60
  78.1 10.2 %fusion.27 = (bf16[4,255,512]{2,1,0:T(8,128)(2,1)S(1)}, bf16[4,255,512]{2,1,0:T(8,128)(2,1)}) fusion(bf16[4,255,512]{2,0,1:T(4,128)(2,1)} %param.15, f32[4,255]{1,0:T(4,128)S(1)} %fusion.47, bf16[512,1536]{1,0:T(8,128)(2,1)} %all-gather.3.cloned.1.call-done, bf16[4,255,512]{2,1,0:T(8,128)(2,1)} %get-tuple-element.41, bf16[4,255,512]{2,1,0:T(8,128)(2,1)S(1)} %bitcast.55, ...), kind=kOutput, calls=%fused_computation.53 | convolution fusion | flops 1654456320 | bytes 7843824 | tf_op jit(solution)/shard_map/dot_general | solution.py:120
  88.3 3.5 %convolution_bitcast_fusion.1 = f32[512,1536]{1,0:T(8,128)} fusion(bf16[4,255,512]{2,1,0:T(8,128)(2,1)S(1)} %get-tuple-element.36, bf16[4,255,512]{2,1,0:T(8,128)(2,1)S(1)} %copy-done.4, bf16[4,255,512]{2,1,0:T(8,128)(2,1)S(1)} %bitcast.56, bf16[4,255,512]{2,1,0:T(8,128)(2,1)S(1)} %get-tuple-element.40), kind=kOutput, calls=%fused_computation.40 | convolution fusion | flops 1613721600 | bytes 7323648 | tf_op jit(solution)/shard_map/dot_general | solution.py:140
  92.0 3.1 %copy.53 = bf16[4,255,512]{2,0,1:T(4,128)(2,1)} copy(bf16[4,255,512]{2,1,0:T(8,128)(2,1)} %get-tuple-element.37) | data formatting | bytes 2088960
  97.3 1.0 pad_bitcast_fusion
  99.0 5.2 %copy.52 = f32[4,256,2,512]{3,2,1,0:T(2,128)} copy(f32[4,256,2,512]{3,1,0,2:T(8,128)S(1)} %pad_maximum_fusion) | data formatting | bytes 8388608 | tf_op jit(solution)/shard_map/stack | solution.py:38
  104.2 6.1 %reshape.329 = f32[4,512,512]{2,1,0:T(8,128)} reshape(f32[4,256,2,512]{3,2,1,0:T(2,128)} %copy.52) | data formatting | bytes 8388608 | tf_op jit(solution)/shard_map/reshape | solution.py:38
  110.3 6.1 %multiply_reduce_fusion.1 = (f32[4,512]{1,0:T(4,128)S(1)}, f32[512]{0:T(512)S(1)}, f32[4,512]{1,0:T(4,128)S(1)}, f32[512]{0:T(512)S(1)}, f32[4,511,512]{2,1,0:T(8,128)S(1)}) fusion(f32[4,511,512]{2,1,0:T(8,128)} %copy-done.1, f32[512]{0:T(512)S(1)} %copy-done.6, f32[4,512]{1,0:T(4,128)S(1)} %add_rsqrt_fusion, f32[4,512]{1,0:T(4,128)S(1)} %broadcast_divide_fusion.2, ...), kind=kLoop, calls=%fused_computation.15 | loop fusion | flops 21971968 | bytes 12607472 | tf_op jit(solution)/shard_map/reduce_sum | solution.py:154
  116.4 1.3 fusion.38
  117.8 40.1 %psum.15 = f32[512,12]{0,1:T(8,128)S(1)} all-reduce(f32[512,12]{0,1:T(8,128)S(1)} %pad_maximum_fusion.7), channel_id=1, replica_groups=mesh['dp'=8,'group'=4] {'dp','group'}, use_global_device_ids=true, to_apply=%region_11.12 | all-reduce | flops 6144 | bytes 49152 | tf_op jit(solution)/shard_map/psum | solution.py:165
  158.6 9.3 %reduce-scatter.2.cloned.1.call-done = f32[64,1536]{1,0:T(8,128)} async-done(((f32[512,1536]{1,0:T(8,128)}), f32[64,1536]{1,0:T(8,128)}) %reduce-scatter.2.cloned.1.call-update) | async-done | bytes 393232 | tf_op jit(solution)/shard_map/reduce_scatter | solution.py:139
  168.5 33.6 %all-reduce.9.cloned.1.call-done = f32[64,1536]{1,0:T(8,128)} async-done(((f32[64,1536]{1,0:T(8,128)}), f32[64,1536]{1,0:T(8,128)}) %all-reduce.9.cloned.1.call-update) | async-done | bytes 393232 | tf_op jit(solution)/shard_map/psum | solution.py:147
  202.1 1.8 copy.72
  (66 shorter events, 10.4 us)
Async XLA Ops:
  7.2 11.1 %copy-start = (bf16[4,2560]{1,0:T(4,128)(2,1)S(1)}, bf16[4,2560]{1,0:T(4,128)(2,1)}, u32[]{:S(2)}) copy-start(bf16[4,2560]{1,0:T(4,128)(2,1)} %param.8) | copy-start | bytes 61444
  7.2 70.9 %all-gather.3.cloned.1.call-start = ((), (), s32[]{:S(2)}) async-start(), calls=%async_computation.2 | async-start | bytes 1769472 | tf_op jit(solution)/shard_map/all_gather | solution.py:119
  19.1 35.8 %all-to-all-start = ((bf16[4,2,2560]{2,1,0:T(2,128)(2,1)}), bf16[4,2,2560]{2,1,0:T(2,128)(2,1)S(1)}, u32[]{:S(2)}, u32[]{:S(2)}) async-start(bf16[4,2,2560]{2,1,0:T(2,128)(2,1)} %copy.42), calls=%async_computation | async-start | bytes 81920 | tf_op jit(solution)/shard_map/all_to_all | solution.py:81
  22.4 145.6 %reduce-scatter.2.cloned.1.call-start = ((), (), s32[]{:S(2)}) async-start(), calls=%async_computation.3 | async-start | bytes 3538944 | tf_op jit(solution)/shard_map/reduce_scatter | solution.py:139
  56.7 1.9 copy-start.5
  56.8 1.9 copy-start.6
  57.8 11.1 %copy-start.1 = (f32[4,511,512]{2,1,0:T(8,128)}, f32[4,511,512]{2,1,0:T(8,128)S(1)}, u32[]{:S(2)}) copy-start(f32[4,511,512]{2,1,0:T(8,128)S(1)} %get-tuple-element.51) | copy-start | bytes 12558340
  78.1 10.2 %copy-start.4 = (bf16[4,255,512]{2,1,0:T(8,128)(2,1)S(1)}, bf16[4,255,512]{2,1,0:T(8,128)(2,1)}, u32[]{:S(2)}) copy-start(bf16[4,255,512]{2,1,0:T(8,128)(2,1)} %get-tuple-element.41) | copy-start | bytes 3133444
  91.8 3.4 %copy-start.3 = (bf16[512,1536]{1,0:T(8,128)(2,1)S(1)}, bf16[512,1536]{1,0:T(8,128)(2,1)}, u32[]{:S(2)}) copy-start(bf16[512,1536]{1,0:T(8,128)(2,1)} %all-gather.3.cloned.1.call-done) | copy-start | bytes 4718596
  91.8 110.3 %all-reduce.9.cloned.1.call-start = ((), (), s32[]{:S(2)}) async-start(), calls=%async_computation.4 | async-start | bytes 786432 | tf_op jit(solution)/shard_map/psum | solution.py:147
  110.3 6.1 %copy-start.2 = (f32[4,511,512]{2,1,0:T(8,128)S(1)}, f32[4,511,512]{2,1,0:T(8,128)}, u32[]{:S(2)}) copy-start(f32[4,511,512]{2,1,0:T(8,128)} %copy-done.1) | copy-start | bytes 12558340
Sparse Core Ops, SparseCore 0:
  10.2 47.2 all-gather.2
  91.9 75.9 reduce-scatter.1
  170.3 31.7 all-reduce.8
where the time goes:
time: 211 us; the launch traced here: 210 us
  blocking collectives  78 us (37%)
  waiting for transfers between devices  43.6 us (21%)
  local copies, waits for them, and re-layouts  32.4 us (15%)
  other arithmetic  19.6 us (9%)
  matrix products  18.5 us (9%)
  between operations  14.7 us (7%)
  starting transfers between devices  3.57 us (2%)
    psum x1, blocking collectives, local(): summed = lax.psum(stacked, ('dp', 'group'))  40.1 us
    psum x1, waiting for transfers between devices, local(): grad_conv = lax.psum(share, 'group')  33.6 us
    all_gather x1, blocking collectives, local(): first_whole = lax.all_gather(first_weight, 'dp', axis=0, tiled=True)  31.5 us
    convert_element_type x1, other arithmetic, local(): (jax.nn.gelu(shifted, approximate=False) * valid_first).astype(jnp.bfloat16)  10.2 us
    dot_general x1, matrix products, local(): lax.dot_general(taps_second, conv_whole, (((1,), (1,)), ((), ())), prefer...  10.2 us
    reduce_scatter x1, waiting for transfers between devices, local(): lax.psum_scatter(lax.dot_general(delta_flat, taps_second, (((0,), (0,)),...  9.35 us
    unnamed x26, local copies, waits for them, and re-layouts  9.01 us
    unnamed x1, blocking collectives  6.38 us
  transfers between devices with their start and end apart: 4, of which 2 were waited for; matrix products, arithmetic and copies ran while one was open for 26% of the time, Pallas kernels for 0%

commit v1 on v0

--- a/solution.py
+++ b/solution.py
@@ -144,7 +144,8 @@
         scatter_dimension=0,
         tiled=True,
     )
-    grad_conv = lax.psum(share, "group")
+    parts = lax.all_gather(share, "group", axis=0, tiled=False)
+    grad_conv = parts.sum(axis=0)
     delta_hidden = spread_back(back_taps, row_count, frames_second, frames_first)
     delta_norm = delta_hidden * valid_first * gelu_slope(shifted)
     gain_term = jnp.sum(delta_norm * normed, axis=(0, 1))

time: 211 us -> 239 us (1.13)
  waiting for transfers between devices: 43.6 us -> 69 us
  other arithmetic: 19.6 us -> 24.4 us
    reduce_scatter x1, waiting for transfers between devices: 9.35 us -> 68.2 us  [local(): lax.psum_scatter(lax.dot_general(delta_flat, taps_second, (((0,), (0,)),...]
    psum x1 -> x0, waiting for transfers between devices: 33.6 us -> none  [local(): grad_conv = lax.psum(share, 'group')]
    another operation x2, other arithmetic: 1.71 us -> 4.3 us  [spread_back(): jnp.stack([even_half, odd_half], axis=2)]
    unnamed x26 -> x25, local copies, waits for them, and re-layouts: 9.01 us -> 7.25 us
  transfers between devices with their start and end apart: 4 -> 4, of which waited for: 2 -> 1; matrix products, arithmetic and copies ran while one was open for 26% -> 24% of each run, Pallas kernels for 0% -> 0%
where the time goes in v1:
time: 239 us
  blocking collectives  77.8 us (33%)
  waiting for transfers between devices  69 us (29%)
  local copies, waits for them, and re-layouts  30.7 us (13%)
  other arithmetic  24.4 us (10%)
  matrix products  18.5 us (8%)
  between operations  14.7 us (6%)
  starting transfers between devices  3.57 us (1%)
    reduce_scatter x1, waiting for transfers between devices, local(): lax.psum_scatter(lax.dot_general(delta_flat, taps_second, (((0,), (0,)),...  68.2 us
    psum x1, blocking collectives, local(): summed = lax.psum(stacked, ('dp', 'group'))  39.9 us
    all_gather x1, blocking collectives, local(): first_whole = lax.all_gather(first_weight, 'dp', axis=0, tiled=True)  31.5 us
    convert_element_type x1, other arithmetic, local(): (jax.nn.gelu(shifted, approximate=False) * valid_first).astype(jnp.bfloat16)  10.2 us
    dot_general x1, matrix products, local(): lax.dot_general(taps_second, conv_whole, (((1,), (1,)), ((), ())), prefer...  10.2 us
    unnamed x25, local copies, waits for them, and re-layouts  7.25 us
    unnamed x1, blocking collectives  6.38 us
    reshape x1, local copies, waits for them, and re-layouts, spread_back(): jnp.stack([even_half, odd_half], axis=2)  6.07 us
  transfers between devices with their start and end apart: 4, of which 1 were waited for; matrix products, arithmetic and copies ran while one was open for 24% of the time, Pallas kernels for 0%

profile of v1, /device:TPU:0, one launch (start us, length us, event | category | flops | bytes accessed | tf_op | source)
XLA Modules:
  0.0 238.5 jit_solution(15657518686597699921)
XLA Ops:
  7.9 1.2 dynamic-slice
  9.8 0.9 dynamic-update-slice
  11.5 6.4 %all-reduce.6 = (s32[16]{0:T(128)S(1)}, s32[16]{0:T(128)S(1)}) all-reduce(s32[16]{0:T(128)S(1)} %dynamic-update-slice, s32[16]{0:T(128)S(1)} %dynamic-update-slice.1), channel_id=1, replica_groups=mesh['dp'=8,'group'=4] {'group'}, use_global_device_ids=true, to_apply=%add.4 | all-reduce | flops 32 | bytes 256
  19.1 3.3 %all-to-all-start = ((bf16[4,2,2560]{2,1,0:T(2,128)(2,1)}), bf16[4,2,2560]{2,1,0:T(2,128)(2,1)S(1)}, u32[]{:S(2)}, u32[]{:S(2)}) async-start(bf16[4,2,2560]{2,1,0:T(2,128)(2,1)} %copy.42), calls=%async_computation | async-start | bytes 81920 | tf_op jit(solution)/shard_map/all_to_all | solution.py:81
  23.2 31.5 %all-gather.1 = bf16[8,64,10]{1,2,0:T(8,128)(2,1)S(1)} all-gather(bf16[1,64,10]{1,2,0:T(8,128)(2,1)} %bitcast.62), channel_id=1, replica_groups=mesh['dp'=8,'group'=4] {'dp'}, dimensions={0}, use_global_device_ids=true | all-gather | bytes 11520 | tf_op jit(solution)/shard_map/all_gather | solution.py:91
  55.1 1.0 reshape.327
  56.8 1.0 multiply_reduce_fusion.3
  58.7 10.2 %fusion.3 = bf16[4,511,512]{2,1,0:T(8,128)(2,1)S(1)} fusion(f32[4,511,512]{2,1,0:T(8,128)S(1)} %get-tuple-element.51, f32[512]{0:T(512)S(1)} %copy-done.5, f32[512]{0:T(512)S(1)} %copy-done.6, f32[4,512]{1,0:T(4,128)S(1)} %add_rsqrt_fusion, f32[4,512]{1,0:T(4,128)S(1)} %broadcast_divide_fusion.2, f32[4,511]{1,0:T(4,128)S(1)} %fusion.46), kind=kLoop, calls=%fused_computation.5 | loop fusion | flops 73256960 | bytes 6307824 | tf_op jit(solution)/shard_map/convert_element_type | solution.py:117
  68.9 1.5 concatenate.22
  70.4 2.7 %reshape.328 = bf16[4,256,2,512]{3,2,1,0:T(2,128)(2,1)S(1)} reshape(bf16[4,512,512]{2,1,0:T(8,128)(2,1)} %concatenate.22) | data formatting | bytes 4194304 | tf_op jit(solution)/shard_map/reshape | solution.py:17
  73.2 3.0 %fusion.59 = (bf16[4,256,1,512]{3,2,1,0:T(2,128)(2,1)S(1)}, bf16[4,256,1,512]{3,2,1,0:T(2,128)(2,1)S(1)}) fusion(bf16[4,256,2,512]{3,2,1,0:T(2,128)(2,1)S(1)} %reshape.328), kind=kLoop, calls=%fused_computation.134 | loop fusion | bytes 4194304 | tf_op jit(solution)/shard_map/slice | solution.py:21
  76.7 1.3 fusion.60
  78.0 10.2 %fusion.27 = (bf16[4,255,512]{2,1,0:T(8,128)(2,1)S(1)}, bf16[4,255,512]{2,1,0:T(8,128)(2,1)}) fusion(bf16[4,255,512]{2,0,1:T(4,128)(2,1)} %param.15, f32[4,255]{1,0:T(4,128)S(1)} %fusion.47, bf16[512,1536]{1,0:T(8,128)(2,1)} %all-gather.5.cloned.1.call-done, bf16[4,255,512]{2,1,0:T(8,128)(2,1)} %get-tuple-element.41, bf16[4,255,512]{2,1,0:T(8,128)(2,1)S(1)} %bitcast.57, ...), kind=kOutput, calls=%fused_computation.53 | convolution fusion | flops 1654456320 | bytes 7843824 | tf_op jit(solution)/shard_map/dot_general | solution.py:120
  88.2 3.5 %convolution_bitcast_fusion.1 = f32[512,1536]{1,0:T(8,128)} fusion(bf16[4,255,512]{2,1,0:T(8,128)(2,1)S(1)} %get-tuple-element.36, bf16[4,255,512]{2,1,0:T(8,128)(2,1)S(1)} %copy-done.4, bf16[4,255,512]{2,1,0:T(8,128)(2,1)S(1)} %bitcast.58, bf16[4,255,512]{2,1,0:T(8,128)(2,1)S(1)} %get-tuple-element.40), kind=kOutput, calls=%fused_computation.40 | convolution fusion | flops 1613721600 | bytes 7323648 | tf_op jit(solution)/shard_map/dot_general | solution.py:140
  92.0 3.1 %copy.53 = bf16[4,255,512]{2,0,1:T(4,128)(2,1)} copy(bf16[4,255,512]{2,1,0:T(8,128)(2,1)} %get-tuple-element.37) | data formatting | bytes 2088960
  97.3 2.2 pad_bitcast_fusion
  99.4 68.2 %reduce-scatter.2.cloned.1.call-done = f32[64,1536]{1,0:T(8,128)} async-done(((f32[512,1536]{1,0:T(8,128)}), f32[64,1536]{1,0:T(8,128)}) %reduce-scatter.2.cloned.1.call-update) | async-done | bytes 393232 | tf_op jit(solution)/shard_map/reduce_scatter | solution.py:139
  167.7 2.1 pad_maximum_fusion
  169.8 5.2 %copy.52 = f32[4,256,2,512]{3,2,1,0:T(2,128)} copy(f32[4,256,2,512]{3,1,0,2:T(8,128)S(1)} %pad_maximum_fusion) | data formatting | bytes 8388608 | tf_op jit(solution)/shard_map/stack | solution.py:38
  175.0 6.1 %reshape.329 = f32[4,512,512]{2,1,0:T(8,128)} reshape(f32[4,256,2,512]{3,2,1,0:T(2,128)} %copy.52) | data formatting | bytes 8388608 | tf_op jit(solution)/shard_map/reshape | solution.py:38
  181.1 6.0 %multiply_reduce_fusion.1 = (f32[4,512]{1,0:T(4,128)S(1)}, f32[512]{0:T(512)S(1)}, f32[4,512]{1,0:T(4,128)S(1)}, f32[512]{0:T(512)S(1)}, f32[4,511,512]{2,1,0:T(8,128)S(1)}) fusion(f32[4,511,512]{2,1,0:T(8,128)} %copy-done.1, f32[512]{0:T(512)S(1)} %copy-done.6, f32[4,512]{1,0:T(4,128)S(1)} %add_rsqrt_fusion, f32[4,512]{1,0:T(4,128)S(1)} %broadcast_divide_fusion.2, ...), kind=kLoop, calls=%fused_computation.15 | loop fusion | flops 21971968 | bytes 12607472 | tf_op jit(solution)/shard_map/reduce_sum | solution.py:155
  187.2 1.3 fusion.38
  188.5 39.9 %psum.7 = f32[512,12]{0,1:T(8,128)S(1)} all-reduce(f32[512,12]{0,1:T(8,128)S(1)} %pad_maximum_fusion.7), channel_id=1, replica_groups=mesh['dp'=8,'group'=4] {'dp','group'}, use_global_device_ids=true, to_apply=%region_11.12 | all-reduce | flops 6144 | bytes 49152 | tf_op jit(solution)/shard_map/psum | solution.py:166
  229.7 2.3 reduce_sum.95
  (66 shorter events, 9.7 us)
Async XLA Ops:
  7.2 11.1 %copy-start = (bf16[4,2560]{1,0:T(4,128)(2,1)S(1)}, bf16[4,2560]{1,0:T(4,128)(2,1)}, u32[]{:S(2)}) copy-start(bf16[4,2560]{1,0:T(4,128)(2,1)} %param.8) | copy-start | bytes 61444
  7.2 70.8 %all-gather.5.cloned.1.call-start = ((), (), s32[]{:S(2)}) async-start(), calls=%async_computation.2 | async-start | bytes 1769472 | tf_op jit(solution)/shard_map/all_gather | solution.py:119
  19.1 35.8 %all-to-all-start = ((bf16[4,2,2560]{2,1,0:T(2,128)(2,1)}), bf16[4,2,2560]{2,1,0:T(2,128)(2,1)S(1)}, u32[]{:S(2)}, u32[]{:S(2)}) async-start(bf16[4,2,2560]{2,1,0:T(2,128)(2,1)} %copy.42), calls=%async_computation | async-start | bytes 81920 | tf_op jit(solution)/shard_map/all_to_all | solution.py:81
  22.4 145.3 %reduce-scatter.2.cloned.1.call-start = ((), (), s32[]{:S(2)}) async-start(), calls=%async_computation.3 | async-start | bytes 3538944 | tf_op jit(solution)/shard_map/reduce_scatter | solution.py:139
  56.7 1.9 copy-start.5
  56.8 1.9 copy-start.6
  57.8 11.1 %copy-start.1 = (f32[4,511,512]{2,1,0:T(8,128)}, f32[4,511,512]{2,1,0:T(8,128)S(1)}, u32[]{:S(2)}) copy-start(f32[4,511,512]{2,1,0:T(8,128)S(1)} %get-tuple-element.51) | copy-start | bytes 12558340
  78.0 10.2 %copy-start.4 = (bf16[4,255,512]{2,1,0:T(8,128)(2,1)S(1)}, bf16[4,255,512]{2,1,0:T(8,128)(2,1)}, u32[]{:S(2)}) copy-start(bf16[4,255,512]{2,1,0:T(8,128)(2,1)} %get-tuple-element.41) | copy-start | bytes 3133444
  91.8 3.4 %copy-start.3 = (bf16[512,1536]{1,0:T(8,128)(2,1)S(1)}, bf16[512,1536]{1,0:T(8,128)(2,1)}, u32[]{:S(2)}) copy-start(bf16[512,1536]{1,0:T(8,128)(2,1)} %all-gather.5.cloned.1.call-done) | copy-start | bytes 4718596
  91.8 138.0 %all-gather.7.cloned.1.call-start = ((), (), s32[]{:S(2)}) async-start(), calls=%async_computation.4 | async-start | bytes 1966080 | tf_op jit(solution)/shard_map/all_gather | solution.py:147
  181.1 6.1 %copy-start.2 = (f32[4,511,512]{2,1,0:T(8,128)S(1)}, f32[4,511,512]{2,1,0:T(8,128)}, u32[]{:S(2)}) copy-start(f32[4,511,512]{2,1,0:T(8,128)} %copy-done.1) | copy-start | bytes 12558340
Sparse Core Ops, SparseCore 0:
  10.2 47.2 all-gather.4
  91.9 75.7 reduce-scatter.1
  169.2 18.7 all-gather.6
